TPU v7x, 32 devices: a whole 2x2x4 slice. The times are simulated.
32 devices in a mesh: row: 4 (over y, x), col: 8 (over z, core).
Axes of the slice: x: 2, y: 2, z: 4, core: 2. Of those that a mesh axis runs over, the one named last changes fastest.
Arguments:
- points: bfloat16 [8192, 256], P(('row', 'col')), may hold values from -0.4 to 0.4, as said below
- spread: float32 [8192], P(('row', 'col')), may hold values from 1 to 12
- vectors: bfloat16 [8192, 64], P(('row', 'col')), may hold values from -6 to 6
Outputs:
- product: float32 [8192, 64], P(('row', 'col'))
Inputs may be any that keep to these rules, and one draw needn't show every extreme that they name: `points`: embedding entries are real values of order 0.1.
All inputs are finite; a program needn't handle non-finite values.
Results may differ from a plain program's by a relative error of at most 0.0085.
Values may be sent and summed in bfloat16 or wider, within the bound.
A program may use at most 128 MiB of HBM per device.

v0:
```python
import jax
import jax.numpy as jnp
from jax import lax
from jax.sharding import PartitionSpec as P


def distances(left_pts, right_pts):
    left_f = left_pts.astype(jnp.float32)
    right_f = right_pts.astype(jnp.float32)
    left_sq = jnp.sum(left_f * left_f, axis=1)
    right_sq = jnp.sum(right_f * right_f, axis=1)
    cross = lax.dot_general(
        left_pts, right_pts, (((1,), (1,)), ((), ())), preferred_element_type=jnp.float32
    )
    return left_sq[:, None] + right_sq[None, :] - 2.0 * cross


def local(points, spread, vectors):
    share_rows = points.shape[0]
    n_rows = lax.axis_size("row")
    n_cols = lax.axis_size("col")
    row_pos = lax.axis_index("row")
    col_pos = lax.axis_index("col")
    blk_pts, blk_bw, blk_vec = (
        lax.all_gather(points, "col", axis=0, tiled=True),
        lax.all_gather(spread.astype(jnp.bfloat16), "col", axis=0, tiled=True).astype(spread.dtype),
        lax.all_gather(vectors, "col", axis=0, tiled=True),
    )
    crs_pts, crs_bw, crs_vec = (
        lax.all_gather(points, "row", axis=0, tiled=True),
        lax.all_gather(spread.astype(jnp.bfloat16), "row", axis=0, tiled=True).astype(spread.dtype),
        lax.all_gather(vectors, "row", axis=0, tiled=True),
    )
    blk_local = jnp.arange(share_rows * n_cols, dtype=jnp.int32)
    blk_ids = row_pos * (n_cols * share_rows) + blk_local
    crs_local = jnp.arange(share_rows * n_rows, dtype=jnp.int32)
    crs_ids = (
        crs_local // share_rows * (n_cols * share_rows)
        + col_pos * share_rows
        + crs_local % share_rows
    )
    same = blk_ids[:, None] == crs_ids[None, :]
    dist = distances(blk_pts, crs_pts)
    kernel = jnp.where(same, jnp.float32(0.0), jnp.exp(-blk_bw[:, None] * dist))
    totals = lax.psum(jnp.sum(kernel, axis=1), "col")
    norm = (kernel / totals[:, None]).astype(jnp.bfloat16)
    to_cross = lax.dot_general(
        norm, blk_vec, (((0,), (0,)), ((), ())), preferred_element_type=jnp.float32
    )
    mirror = jnp.where(same, jnp.float32(0.0), jnp.exp(-crs_bw[None, :] * dist))
    mirror_tot = lax.psum(jnp.sum(mirror, axis=0), "row")
    mirror_norm = (mirror / mirror_tot[None, :]).astype(jnp.bfloat16)
    to_cross = to_cross + lax.dot_general(
        mirror_norm, blk_vec, (((0,), (0,)), ((), ())), preferred_element_type=jnp.float32
    )
    summed = lax.psum_scatter(to_cross, "row", scatter_dimension=0, tiled=True)
    return 0.5 * summed


def solution(mesh):
    placed = (P(("row", "col"), None), P(("row", "col")), P(("row", "col"), None))
    return jax.shard_map(
        local, mesh=mesh, in_specs=placed, out_specs=P(("row", "col"), None), check_vma=False
    )
```

profile of v0, /device:TPU:0, one launch (start us, length us, event | category | flops | bytes accessed | tf_op | source)
XLA Modules:
  0.0 126.9 jit_solution(6512187139585747209)
XLA Ops:
  6.5 0.0 all-gather.4.cloned.1.call-start
  6.5 0.7 all-gather.4.cloned.1.call-update
  7.3 0.0 reduce-scatter.2.cloned.1.call-start
  7.3 0.7 convert_element_type.22
  8.0 9.5 %all-gather.1 = bf16[4,1,256]{2,1,0:T(2,128)(2,1)S(1)} all-gather(bf16[1,1,256]{2,1,0:T(2,128)(2,1)S(1)} %reshape.35), channel_id=1, replica_groups=mesh['row'=4,'col'=8] {'row'}, dimensions={0}, use_global_device_ids=true | all-gather | bytes 2560 | tf_op jit(solution)/shard_map/all_gather | solution.py:31
  17.5 12.0 %all-gather = bf16[8,1,256]{2,1,0:T(2,128)(2,1)S(1)} all-gather(bf16[1,1,256]{2,1,0:T(2,128)(2,1)S(1)} %reshape.35), channel_id=1, replica_groups=mesh['row'=4,'col'=8] {'col'}, dimensions={0}, use_global_device_ids=true | all-gather | bytes 4608 | tf_op jit(solution)/shard_map/all_gather | solution.py:26
  29.5 10.3 %all_gather.17 = bf16[1024,256]{1,0:T(8,128)(2,1)S(1)} all-gather(bf16[256,256]{1,0:T(8,128)(2,1)} %param.3), channel_id=1, replica_groups=mesh['row'=4,'col'=8] {'row'}, dimensions={0}, use_global_device_ids=true | all-gather | bytes 655360 | tf_op jit(solution)/shard_map/all_gather | solution.py:30
  39.8 14.4 %all_gather.18 = bf16[2048,64]{0,1:T(8,128)(2,1)S(1)} all-gather(bf16[256,64]{0,1:T(8,128)(2,1)} %param.5), channel_id=1, replica_groups=mesh['row'=4,'col'=8] {'col'}, dimensions={0}, use_global_device_ids=true | all-gather | bytes 294912 | tf_op jit(solution)/shard_map/all_gather | solution.py:27
  54.2 0.2 multiply_reduce_fusion.1
  54.5 0.0 all-gather.4.cloned.1.call-done
  54.5 1.6 %multiply_reduce_fusion = f32[2048]{0:T(1024)S(1)} fusion(bf16[2048,256]{1,0:T(8,128)(2,1)} %all-gather.4.cloned.1.call-done), kind=kLoop, calls=%fused_computation.9 | loop fusion | flops 1570816 | bytes 1056768 | tf_op jit(solution)/shard_map/reduce_sum | solution.py:10
  56.1 7.5 %fusion = (f32[2048]{0:T(1024)S(1)}, f32[1024]{0:T(1024)S(1)}, f32[2048,1024]{1,0:T(8,128)}) fusion(f32[1024]{0:T(1024)S(1)} %multiply_reduce_fusion.1, f32[2048]{0:T(1024)S(1)} %multiply_reduce_fusion, f32[2048]{0:T(1024)S(1)} %bitcast.6, s32[1024]{0:T(1024)S(1)} %fusion.13, s32[2048]{0:T(1024)S(1)} %iota_add_fusion, f32[1024]{0:T(1024)S(1)} %bitcast.8, ...), kind=kOutput, calls=%fused_computation.5 | convolution fusion | flops 1094710272 | bytes 10010624 | tf_op jit(solution)/shard_map/dot_general | solution.py:12
  63.6 8.9 %psum.15 = f32[1024]{0:T(1024)S(1)} all-reduce(f32[1024]{0:T(1024)S(1)} %get-tuple-element.6), channel_id=1, replica_groups=mesh['row'=4,'col'=8] {'row'}, use_global_device_ids=true, to_apply=%region_5.6 | all-reduce | flops 1024 | bytes 8192 | tf_op jit(solution)/shard_map/psum | solution.py:51
  72.5 13.9 %psum.14 = f32[2048]{0:T(1024)S(1)} all-reduce(f32[2048]{0:T(1024)S(1)} %get-tuple-element.5), channel_id=1, replica_groups=mesh['row'=4,'col'=8] {'col'}, use_global_device_ids=true, to_apply=%region_3.4 | all-reduce | flops 2048 | bytes 16384 | tf_op jit(solution)/shard_map/psum | solution.py:45
  86.4 0.0 copy-start
  86.4 6.9 %fusion.2 = f32[1024,64]{0,1:T(8,128)S(1)} fusion(bf16[2048,64]{0,1:T(8,128)(2,1)S(1)} %all_gather.18, f32[2048,1024]{1,0:T(8,128)} %get-tuple-element.7, f32[1024]{0:T(1024)S(1)} %psum.15, f32[1024]{0:T(1024)S(1)} %bitcast.9, f32[1024]{0:T(1024)S(1)} %multiply_reduce_fusion.1, f32[2048]{0:T(1024)S(1)} %multiply_reduce_fusion, s32[1024]{0:T(1024)S(1)} %fusion.13, ...), kind=kOutput, calls=%fused_computation.7 | convolution fusion | flops 285212672 | bytes 8945664 | tf_op jit(solution)/shard_map/dot_general | solution.py:53
  93.3 0.0 copy-done
  93.3 3.8 %fusion.4 = f32[1024,64]{0,1:T(8,128)} fusion(f32[1024,64]{0,1:T(8,128)S(1)} %fusion.2, bf16[2048,64]{0,1:T(8,128)(2,1)S(1)} %all_gather.18, f32[2048,1024]{1,0:T(8,128)S(1)} %copy-done, f32[2048]{0:T(1024)S(1)} %psum.14, f32[1024]{0:T(1024)S(1)} %multiply_reduce_fusion.1, f32[2048]{0:T(1024)S(1)} %multiply_reduce_fusion, f32[2048]{0:T(1024)S(1)} %bitcast.7, ...), kind=kOutput, calls=%fused_computation.10 | convolution fusion | flops 285278208 | bytes 9216000 | tf_op jit(solution)/shard_map/dot_general | solution.py:47
  97.1 0.0 reduce-scatter.2.cloned.1.call-update
  97.2 21.5 %reduce-scatter.2.cloned.1.call-done = f32[256,64]{0,1:T(8,128)} async-done(((f32[1024,64]{0,1:T(8,128)}), f32[256,64]{0,1:T(8,128)}) %reduce-scatter.2.cloned.1.call-update) | async-done | bytes 65552 | tf_op jit(solution)/shard_map/reduce_scatter | solution.py:56
  118.6 1.5 %broadcast_multiply_fusion = f32[256,64]{0,1:T(8,128)} fusion(f32[256,64]{0,1:T(8,128)} %reduce-scatter.2.cloned.1.call-done), kind=kLoop, calls=%fused_computation.12 | loop fusion | flops 16384 | bytes 131072 | tf_op jit(solution)/shard_map/mul | solution.py:57
  (5 shorter events, 0.0 us)
Async XLA Ops:
  6.5 47.9 %all-gather.4.cloned.1.call-start = ((), (), s32[]{:S(2)}) async-start(), calls=%async_computation.1 | async-start | bytes 1179648 | tf_op jit(solution)/shard_map/all_gather | solution.py:25
  7.3 111.4 %reduce-scatter.2.cloned.1.call-start = ((), (), s32[]{:S(2)}) async-start(), calls=%async_computation.2 | async-start | bytes 327680 | tf_op jit(solution)/shard_map/reduce_scatter | solution.py:56
  86.4 6.9 %copy-start = (f32[2048,1024]{1,0:T(8,128)S(1)}, f32[2048,1024]{1,0:T(8,128)}, u32[]{:S(2)}) copy-start(f32[2048,1024]{1,0:T(8,128)} %get-tuple-element.7) | copy-start | bytes 25165828
Sparse Core Ops, SparseCore 0:
  9.0 24.7 all-gather.3
  97.3 21.3 reduce-scatter.1
where the time goes:
time: 127 us
  blocking collectives  69 us (54%)
  waiting for transfers between devices  22.2 us (17%)
  matrix products  18.2 us (14%)
  between operations  13.5 us (11%)
  other arithmetic  3.97 us (3%)
    reduce_scatter x1, waiting for transfers between devices, local(): summed = lax.psum_scatter(to_cross, 'row', scatter_dimension=0, tiled=True)  21.5 us
    all_gather x1, blocking collectives, local(): lax.all_gather(vectors, 'col', axis=0, tiled=True)  14.4 us
    psum x1, blocking collectives, local(): totals = lax.psum(jnp.sum(kernel, axis=1), 'col')  13.9 us
    all_gather x1, blocking collectives, local(): lax.all_gather(spread.astype(jnp.bfloat16), 'col', axis=0, tiled=True)  12 us
    all_gather x1, blocking collectives, local(): lax.all_gather(points, 'row', axis=0, tiled=True)  10.3 us
    all_gather x1, blocking collectives, local(): lax.all_gather(spread.astype(jnp.bfloat16), 'row', axis=0, tiled=True)  9.5 us
    psum x1, blocking collectives, local(): mirror_tot = lax.psum(jnp.sum(mirror, axis=0), 'row')  8.9 us
    dot_general x1, matrix products, distances(): lax.dot_general(left_pts, right_pts, (((1,), (1,)), ((), ())), preferred_...  7.5 us
  transfers between devices with their start and end apart: 2, of which 1 were waited for; matrix products, arithmetic and copies ran while one was open for 1% of the time, Pallas kernels for 0%

commit v1 on v0

--- a/solution.py
+++ b/solution.py
@@ -21,9 +21,42 @@
     n_cols = lax.axis_size("col")
     row_pos = lax.axis_index("row")
     col_pos = lax.axis_index("col")
+
+    def assign_widths(panel):
+        w_next, long_array, state_next = (
+            lax.axis_size("col"),
+            lax.axis_index("col"),
+            panel.shape[0],
+        )
+        reply = lax.dynamic_update_slice_in_dim(
+            jnp.zeros(
+                tuple((kk * w_next if to_i == 0 else kk for to_i, kk in enumerate(panel.shape))),
+                panel.dtype,
+            ),
+            panel,
+            long_array * state_next,
+            axis=0,
+        )
+        extra = wide_out = panel
+        for j in [*range(1, w_next // 2 + 1)]:
+            extra = lax.ppermute(
+                extra, "col", tuple(((to_i, (to_i + 1) % w_next) for to_i in range(w_next)))
+            )
+            reply = lax.dynamic_update_slice_in_dim(
+                reply, extra, (long_array - j) % w_next * state_next, axis=0
+            )
+            if 2 * j < w_next:
+                wide_out = lax.ppermute(
+                    wide_out, "col", tuple(((to_i, (to_i - 1) % w_next) for to_i in range(w_next)))
+                )
+                reply = lax.dynamic_update_slice_in_dim(
+                    reply, wide_out, (long_array + j) % w_next * state_next, axis=0
+                )
+        return reply
+
     blk_pts, blk_bw, blk_vec = (
         lax.all_gather(points, "col", axis=0, tiled=True),
-        lax.all_gather(spread.astype(jnp.bfloat16), "col", axis=0, tiled=True).astype(spread.dtype),
+        assign_widths(spread.astype(jnp.bfloat16)).astype(spread.dtype),
         lax.all_gather(vectors, "col", axis=0, tiled=True),
     )
     crs_pts, crs_bw, crs_vec = (

time: 127 us -> 132 us (1.039)
  blocking collectives: 69 us -> 55.8 us
  starting transfers between devices: 0.04 us -> 11.7 us
  waiting for transfers between devices: 22.2 us -> 27.4 us
  local copies, waits for them, and re-layouts: 0.01 us -> 1.61 us
    all_gather x1 -> x0, blocking collectives: 12 us -> none  [local(): lax.all_gather(spread.astype(jnp.bfloat16), 'col', axis=0, tiled=True)]
    ppermute x0 -> x7, starting transfers between devices: none -> 11.6 us  [the longest x3 10.8 us: assign_widths(): lax.ppermute(wide_out, 'col', tuple(((to_i, (to_i - 1) % w_next) for to_i...]
    ppermute x0 -> x7, waiting for transfers between devices: none -> 5.78 us  [the longest x4 5.77 us: assign_widths(): lax.ppermute(extra, 'col', tuple(((to_i, (to_i + 1) % w_next) for to_i in...]
    dynamic_update_slice x0 -> x8, local copies, waits for them, and re-layouts: none -> 1.6 us  [the longest x4 0.75 us: assign_widths(): lax.dynamic_update_slice_in_dim(reply, extra, (long_array - j) % w_next *...]
  transfers between devices with their start and end apart: 2 -> 9, of which waited for: 1 -> 4; matrix products, arithmetic and copies ran while one was open for 1% -> 2% of each run, Pallas kernels for 0% -> 0%
where the time goes in v1:
time: 132 us
  blocking collectives  55.8 us (42%)
  waiting for transfers between devices  27.4 us (21%)
  matrix products  18.1 us (14%)
  between operations  13.5 us (10%)
  starting transfers between devices  11.7 us (9%)
  other arithmetic  3.96 us (3%)
  local copies, waits for them, and re-layouts  1.61 us (1%)
    reduce_scatter x1, waiting for transfers between devices, local(): summed = lax.psum_scatter(to_cross, 'row', scatter_dimension=0, tiled=True)  20.9 us
    all_gather x1, blocking collectives, local(): lax.all_gather(vectors, 'col', axis=0, tiled=True)  14.4 us
    psum x1, blocking collectives, local(): totals = lax.psum(jnp.sum(kernel, axis=1), 'col')  13.9 us
    ppermute x3, starting transfers between devices, assign_widths(): lax.ppermute(wide_out, 'col', tuple(((to_i, (to_i - 1) % w_next) for to_i...  10.8 us
    all_gather x1, blocking collectives, local(): lax.all_gather(points, 'row', axis=0, tiled=True)  10 us
    psum x1, blocking collectives, local(): mirror_tot = lax.psum(jnp.sum(mirror, axis=0), 'row')  8.89 us
    all_gather x1, blocking collectives, local(): lax.all_gather(spread.astype(jnp.bfloat16), 'row', axis=0, tiled=True)  8.56 us
    dot_general x1, matrix products, distances(): lax.dot_general(left_pts, right_pts, (((1,), (1,)), ((), ())), preferred_...  7.48 us
  transfers between devices with their start and end apart: 9, of which 4 were waited for; matrix products, arithmetic and copies ran while one was open for 2% of the time, Pallas kernels for 0%

profile of v1, /device:TPU:0, one launch (start us, length us, event | category | flops | bytes accessed | tf_op | source)
XLA Modules:
  0.0 132.0 jit_solution(7380711199094519799)
XLA Ops:
  6.5 0.0 all-gather.3.cloned.1.call-start
  6.5 0.7 all-gather.3.cloned.1.call-update
  7.3 0.0 reduce-scatter.2.cloned.1.call-start
  7.3 0.7 convert_element_type.22
  8.0 0.5 collective-permute-start
  8.4 4.0 %collective-permute-start.1 = (bf16[256]{0:T(256)(128)(2,1)S(1)}, bf16[256]{0:T(256)(128)(2,1)S(1)}, u32[]{:S(2)}, u32[]{:S(2)}) collective-permute-start(bf16[256]{0:T(256)(128)(2,1)S(1)} %convert_element_type.22), channel_id=1, source_target_pairs={{0,7},{1,0},{2,1},{3,2},{4,3},{5,4},{6,5},{7,6},{8,15},{9,8},{10,9... | collective-permute-start | bytes 1544 | tf_op jit(solution)/shard_map/ppermute | solution.py:49
  12.5 8.6 %all-gather = bf16[4,1,256]{2,1,0:T(2,128)(2,1)S(1)} all-gather(bf16[1,1,256]{2,1,0:T(2,128)(2,1)S(1)} %reshape.35), channel_id=1, replica_groups=mesh['row'=4,'col'=8] {'row'}, dimensions={0}, use_global_device_ids=true | all-gather | bytes 2560 | tf_op jit(solution)/shard_map/all_gather | solution.py:64
  21.0 10.0 %all_gather.13 = bf16[1024,256]{1,0:T(8,128)(2,1)S(1)} all-gather(bf16[256,256]{1,0:T(8,128)(2,1)} %param.3), channel_id=1, replica_groups=mesh['row'=4,'col'=8] {'row'}, dimensions={0}, use_global_device_ids=true | all-gather | bytes 655360 | tf_op jit(solution)/shard_map/all_gather | solution.py:63
  31.1 14.4 %all_gather.14 = bf16[2048,64]{0,1:T(8,128)(2,1)S(1)} all-gather(bf16[256,64]{0,1:T(8,128)(2,1)} %param.5), channel_id=1, replica_groups=mesh['row'=4,'col'=8] {'col'}, dimensions={0}, use_global_device_ids=true | all-gather | bytes 294912 | tf_op jit(solution)/shard_map/all_gather | solution.py:60
  45.5 0.2 multiply_reduce_fusion.1
  45.7 0.0 collective-permute-done
  45.7 0.4 collective-permute-start.2
  46.1 0.0 collective-permute-done.1
  46.1 3.2 %collective-permute-start.3 = (bf16[256]{0:T(256)(128)(2,1)S(1)}, bf16[256]{0:T(256)(128)(2,1)S(1)}, u32[]{:S(2)}, u32[]{:S(2)}) collective-permute-start(bf16[256]{0:T(256)(128)(2,1)S(1)} %collective-permute-done.1), channel_id=1, source_target_pairs={{0,7},{1,0},{2,1},{3,2},{4,3},{5,4},{6,5},{7,6},{8,15},{9,8},{10,9... | collective-permute-start | bytes 1544 | tf_op jit(solution)/shard_map/ppermute | solution.py:49
  49.3 1.2 collective-permute-done.2
  50.5 0.0 collective-permute-start.4
  50.6 0.2 dynamic_update_slice.24
  50.8 0.0 collective-permute-done.3
  50.8 3.5 %collective-permute-start.5 = (bf16[256]{0:T(256)(128)(2,1)S(1)}, bf16[256]{0:T(256)(128)(2,1)S(1)}, u32[]{:S(2)}, u32[]{:S(2)}) collective-permute-start(bf16[256]{0:T(256)(128)(2,1)S(1)} %collective-permute-done.3), channel_id=1, source_target_pairs={{0,7},{1,0},{2,1},{3,2},{4,3},{5,4},{6,5},{7,6},{8,15},{9,8},{10,9... | collective-permute-start | bytes 1544 | tf_op jit(solution)/shard_map/ppermute | solution.py:49
  54.3 1.0 collective-permute-done.4
  55.3 0.0 collective-permute-start.6
  55.3 0.2 dynamic_update_slice.25
  55.5 0.2 dynamic_update_slice.26
  55.7 0.2 dynamic_update_slice.27
  55.9 0.2 dynamic_update_slice.28
  56.1 0.2 dynamic_update_slice.29
  56.3 0.0 collective-permute-done.5
  56.3 0.2 dynamic_update_slice.30
  56.5 3.6 %collective-permute-done.6 = bf16[256]{0:T(256)(128)(2,1)S(1)} collective-permute-done((bf16[256]{0:T(256)(128)(2,1)S(1)}, bf16[256]{0:T(256)(128)(2,1)S(1)}, u32[]{:S(2)}, u32[]{:S(2)}) %collective-permute-start.6) | collective-permute-done | bytes 544 | tf_op jit(solution)/shard_map/ppermute | solution.py:42
  60.1 0.2 dynamic_update_slice.31
  60.3 0.0 all-gather.3.cloned.1.call-done
  60.3 1.6 %multiply_reduce_fusion = f32[2048]{0:T(1024)S(1)} fusion(bf16[2048,256]{1,0:T(8,128)(2,1)} %all-gather.3.cloned.1.call-done), kind=kLoop, calls=%fused_computation.9 | loop fusion | flops 1570816 | bytes 1056768 | tf_op jit(solution)/shard_map/reduce_sum | solution.py:10
  61.8 7.5 %fusion = (f32[2048]{0:T(1024)S(1)}, f32[1024]{0:T(1024)S(1)}, f32[2048,1024]{1,0:T(8,128)}) fusion(f32[1024]{0:T(1024)S(1)} %multiply_reduce_fusion.1, f32[2048]{0:T(1024)S(1)} %multiply_reduce_fusion, f32[2048]{0:T(1024)S(1)} %convert_negate_fusion, s32[1024]{0:T(1024)S(1)} %fusion.13, s32[2048]{0:T(1024)S(1)} %iota_add_fusion, f32[1024]{0:T(1024)S(1)} %bitcast.5, ...), kind=kOutput, calls=%fused_computation.5 | convolution fusion | flops 1094710272 | bytes 10010624 | tf_op jit(solution)/shard_map/dot_general | solution.py:12
  69.3 8.9 %psum.15 = f32[1024]{0:T(1024)S(1)} all-reduce(f32[1024]{0:T(1024)S(1)} %get-tuple-element.6), channel_id=1, replica_groups=mesh['row'=4,'col'=8] {'row'}, use_global_device_ids=true, to_apply=%region_5.6 | all-reduce | flops 1024 | bytes 8192 | tf_op jit(solution)/shard_map/psum | solution.py:84
  78.2 13.9 %psum.14 = f32[2048]{0:T(1024)S(1)} all-reduce(f32[2048]{0:T(1024)S(1)} %get-tuple-element.5), channel_id=1, replica_groups=mesh['row'=4,'col'=8] {'col'}, use_global_device_ids=true, to_apply=%region_3.4 | all-reduce | flops 2048 | bytes 16384 | tf_op jit(solution)/shard_map/psum | solution.py:78
  92.1 0.0 copy-start
  92.1 6.9 %fusion.2 = f32[1024,64]{0,1:T(8,128)S(1)} fusion(bf16[2048,64]{0,1:T(8,128)(2,1)S(1)} %all_gather.14, f32[2048,1024]{1,0:T(8,128)} %get-tuple-element.7, f32[1024]{0:T(1024)S(1)} %psum.15, f32[1024]{0:T(1024)S(1)} %bitcast.6, f32[1024]{0:T(1024)S(1)} %multiply_reduce_fusion.1, f32[2048]{0:T(1024)S(1)} %multiply_reduce_fusion, s32[1024]{0:T(1024)S(1)} %fusion.13, ...), kind=kOutput, calls=%fused_computation.7 | convolution fusion | flops 285212672 | bytes 8945664 | tf_op jit(solution)/shard_map/dot_general | solution.py:86
  99.1 0.0 copy-done
  99.1 3.7 %fusion.4 = f32[1024,64]{0,1:T(8,128)} fusion(f32[1024,64]{0,1:T(8,128)S(1)} %fusion.2, bf16[2048,64]{0,1:T(8,128)(2,1)S(1)} %all_gather.14, f32[2048,1024]{1,0:T(8,128)S(1)} %copy-done, f32[2048]{0:T(1024)S(1)} %psum.14, f32[1024]{0:T(1024)S(1)} %multiply_reduce_fusion.1, f32[2048]{0:T(1024)S(1)} %multiply_reduce_fusion, f32[2048]{0:T(1024)S(1)} %convert_negate_fusion, ...), kind=kOutput, calls=%fused_computation.10 | convolution fusion | flops 285278208 | bytes 9216000 | tf_op jit(solution)/shard_map/dot_general | solution.py:80
  102.8 0.0 reduce-scatter.2.cloned.1.call-update
  102.8 20.9 %reduce-scatter.2.cloned.1.call-done = f32[256,64]{0,1:T(8,128)} async-done(((f32[1024,64]{0,1:T(8,128)}), f32[256,64]{0,1:T(8,128)}) %reduce-scatter.2.cloned.1.call-update) | async-done | bytes 65552 | tf_op jit(solution)/shard_map/reduce_scatter | solution.py:89
  123.7 1.5 %broadcast_multiply_fusion = f32[256,64]{0,1:T(8,128)} fusion(f32[256,64]{0,1:T(8,128)} %reduce-scatter.2.cloned.1.call-done), kind=kLoop, calls=%fused_computation.12 | loop fusion | flops 16384 | bytes 131072 | tf_op jit(solution)/shard_map/mul | solution.py:90
  (6 shorter events, 0.0 us)
Async XLA Ops:
  6.5 53.7 %all-gather.3.cloned.1.call-start = ((), (), s32[]{:S(2)}) async-start(), calls=%async_computation.1 | async-start | bytes 1179648 | tf_op jit(solution)/shard_map/all_gather | solution.py:58
  7.3 116.5 %reduce-scatter.2.cloned.1.call-start = ((), (), s32[]{:S(2)}) async-start(), calls=%async_computation.2 | async-start | bytes 327680 | tf_op jit(solution)/shard_map/reduce_scatter | solution.py:89
  8.0 37.7 %collective-permute-start = (bf16[256]{0:T(256)(128)(2,1)S(1)}, bf16[256]{0:T(256)(128)(2,1)S(1)}, u32[]{:S(2)}, u32[]{:S(2)}) collective-permute-start(bf16[256]{0:T(256)(128)(2,1)S(1)} %convert_element_type.22), channel_id=1, source_target_pairs={{0,1},{1,2},{2,3},{3,4},{4,5},{5,6},{6,7},{7,0},{8,9},{9,10},{10,1... | collective-permute-start | bytes 1544 | tf_op jit(solution)/shard_map/ppermute | solution.py:42
  8.4 37.7 %collective-permute-start.1 = (bf16[256]{0:T(256)(128)(2,1)S(1)}, bf16[256]{0:T(256)(128)(2,1)S(1)}, u32[]{:S(2)}, u32[]{:S(2)}) collective-permute-start(bf16[256]{0:T(256)(128)(2,1)S(1)} %convert_element_type.22), channel_id=1, source_target_pairs={{0,7},{1,0},{2,1},{3,2},{4,3},{5,4},{6,5},{7,6},{8,15},{9,8},{10,9... | collective-permute-start | bytes 1544 | tf_op jit(solution)/shard_map/ppermute | solution.py:49
  45.7 4.8 %collective-permute-start.2 = (bf16[256]{0:T(256)(128)(2,1)S(1)}, bf16[256]{0:T(256)(128)(2,1)S(1)}, u32[]{:S(2)}, u32[]{:S(2)}) collective-permute-start(bf16[256]{0:T(256)(128)(2,1)S(1)} %collective-permute-done), channel_id=1, source_target_pairs={{0,1},{1,2},{2,3},{3,4},{4,5},{5,6},{6,7},{7,0},{8,9},{9,10},{10,1... | collective-permute-start | bytes 1544 | tf_op jit(solution)/shard_map/ppermute | solution.py:42
  46.1 4.7 %collective-permute-start.3 = (bf16[256]{0:T(256)(128)(2,1)S(1)}, bf16[256]{0:T(256)(128)(2,1)S(1)}, u32[]{:S(2)}, u32[]{:S(2)}) collective-permute-start(bf16[256]{0:T(256)(128)(2,1)S(1)} %collective-permute-done.1), channel_id=1, source_target_pairs={{0,7},{1,0},{2,1},{3,2},{4,3},{5,4},{6,5},{7,6},{8,15},{9,8},{10,9... | collective-permute-start | bytes 1544 | tf_op jit(solution)/shard_map/ppermute | solution.py:49
  50.5 4.8 %collective-permute-start.4 = (bf16[256]{0:T(256)(128)(2,1)S(1)}, bf16[256]{0:T(256)(128)(2,1)S(1)}, u32[]{:S(2)}, u32[]{:S(2)}) collective-permute-start(bf16[256]{0:T(256)(128)(2,1)S(1)} %collective-permute-done.2), channel_id=1, source_target_pairs={{0,1},{1,2},{2,3},{3,4},{4,5},{5,6},{6,7},{7,0},{8,9},{9,10},{10,1... | collective-permute-start | bytes 1544 | tf_op jit(solution)/shard_map/ppermute | solution.py:42
  50.8 5.5 %collective-permute-start.5 = (bf16[256]{0:T(256)(128)(2,1)S(1)}, bf16[256]{0:T(256)(128)(2,1)S(1)}, u32[]{:S(2)}, u32[]{:S(2)}) collective-permute-start(bf16[256]{0:T(256)(128)(2,1)S(1)} %collective-permute-done.3), channel_id=1, source_target_pairs={{0,7},{1,0},{2,1},{3,2},{4,3},{5,4},{6,5},{7,6},{8,15},{9,8},{10,9... | collective-permute-start | bytes 1544 | tf_op jit(solution)/shard_map/ppermute | solution.py:49
  55.3 4.8 %collective-permute-start.6 = (bf16[256]{0:T(256)(128)(2,1)S(1)}, bf16[256]{0:T(256)(128)(2,1)S(1)}, u32[]{:S(2)}, u32[]{:S(2)}) collective-permute-start(bf16[256]{0:T(256)(128)(2,1)S(1)} %collective-permute-done.4), channel_id=1, source_target_pairs={{0,1},{1,2},{2,3},{3,4},{4,5},{5,6},{6,7},{7,0},{8,9},{9,10},{10,1... | collective-permute-start | bytes 1544 | tf_op jit(solution)/shard_map/ppermute | solution.py:42
  92.1 7.0 %copy-start = (f32[2048,1024]{1,0:T(8,128)S(1)}, f32[2048,1024]{1,0:T(8,128)}, u32[]{:S(2)}) copy-start(f32[2048,1024]{1,0:T(8,128)} %get-tuple-element.7) | copy-start | bytes 25165828
Sparse Core Ops, SparseCore 0:
  9.0 24.7 all-gather.2
  103.0 20.7 reduce-scatter.1
